TPU v7x, 32 devices: a whole 2x2x4 slice. The times are simulated.
32 devices in a mesh: aux: 16 (over z, y, x), grp: 2 (over core).
Axes of the slice: x: 2, y: 2, z: 4, core: 2. Of those that a mesh axis runs over, the one named last changes fastest.
Arguments:
- integrals: bfloat16 [1024, 16, 4096], P(('aux', 'grp')), may hold values from -6 to 6
- block_pairs: int32 [32, 16, 2], P(('aux', 'grp')), may hold values from 0 to 63
- occupied: bfloat16 [2, 4096], replicated, may hold values from -0.75 to 0.75
- virtual: bfloat16 [4096, 3072], P(None, 'grp'), may hold values from -0.1875 to 0.1875
- stored: bfloat16 [1024, 6144], P('aux'), may hold values from -0.1875 to 0.1875
Outputs:
- exchange_panel: bfloat16 [2, 3072, 2, 3072], P(None, ('grp', 'aux'))
Inputs may be any that keep to these rules, and one draw needn't show every extreme that they name: `block_pairs`: block pairs may repeat within a shard; repeated blocks add.
All inputs are finite; a program needn't handle non-finite values.
Results may differ from a plain program's by a relative error of at most 0.0095.
Values may be sent and summed in bfloat16 or wider, within the bound.
A program may use at most 192 MiB of HBM per device.

v0:
```python
import jax
import jax.numpy as jnp
from jax import lax
from jax.sharding import PartitionSpec as P

NBAS = 4096
BLK = 64
V = 3072
NOCC = 2
JWIN = 2


def half_transform(integrals, pairs, occupied):
    nblocks = NBAS // BLK
    aux_rows = integrals.shape[0]
    block_count = integrals.shape[1]
    block_iota = jnp.arange(nblocks, dtype=jnp.int32)
    row_pick = (pairs[:, 0:1] == block_iota[None, :]).astype(jnp.float32)
    col_pick = (pairs[:, 1:2] == block_iota[None, :]).astype(jnp.float32)
    occ_blocks = occupied.astype(jnp.float32).reshape(NOCC, nblocks, BLK)
    picked = jnp.einsum("ikm,bk->ibm", occ_blocks, row_pick).astype(jnp.bfloat16)
    squares = integrals.reshape(aux_rows, block_count, BLK, BLK)
    partial_value = jnp.einsum(
        "ibm,pbmn->pibn", picked, squares, preferred_element_type=jnp.float32
    )
    placed = jnp.einsum("pibn,bk->pikn", partial_value, col_pick)
    return placed.reshape(aux_rows, NOCC * NBAS).astype(jnp.bfloat16)


def per_device(integrals, block_pairs, occupied, virtual, stored):
    half = half_transform(integrals, block_pairs[0], occupied)
    slab = virtual.shape[1]
    piece = lax.all_gather(half, "grp", axis=0, tiled=True)
    count = piece.shape[0]
    flat = piece.reshape(count * NOCC, NBAS)
    product = jnp.dot(flat, virtual, preferred_element_type=jnp.float32).astype(jnp.bfloat16)
    factor = product.reshape(count, NOCC, slab).transpose(0, 2, 1).reshape(count, slab * NOCC)
    summed = lax.psum_scatter(
        lax.dot_general(
            factor, stored, (((0,), (0,)), ((), ())), preferred_element_type=jnp.float32
        ),
        "aux",
        scatter_dimension=0,
        tiled=True,
    )
    panel = summed.astype(jnp.bfloat16)
    local_virtuals = panel.shape[0] // NOCC
    shaped = panel.reshape(local_virtuals, NOCC, JWIN, V)
    return shaped.transpose(1, 0, 2, 3)


def solution(mesh):
    in_specs = (
        P(("aux", "grp"), None, None),
        P(("aux", "grp"), None, None),
        P(),
        P(None, "grp"),
        P("aux", None),
    )
    out_specs = P(None, ("grp", "aux"), None, None)
    return jax.shard_map(
        per_device, mesh=mesh, in_specs=in_specs, out_specs=out_specs, check_vma=False
    )
```

profile of v0, /device:TPU:0, one launch (start us, length us, event | category | flops | bytes accessed | tf_op | source)
XLA Modules:
  0.0 1129.1 jit_solution(17778713759737627414)
XLA Ops:
  6.5 0.0 copy-start
  6.5 0.0 all-gather.2.cloned.1.call-start
  6.5 0.8 slice_bitcast_fusion.1
  7.3 0.8 reshape.20
  8.1 12.6 %reshape.21 = bf16[32,16,64,64]{3,2,1,0:T(8,128)(2,1)} reshape(bf16[32,16,4096]{2,1,0:T(8,128)(2,1)} %param.5) | data formatting | bytes 8388608 | tf_op jit(solution)/shard_map/reshape | solution.py:22
  20.7 0.2 convolution_convert_fusion.2
  20.9 4.6 fusion
  25.5 0.6 fusion.2
  26.1 1.6 convert_element_type.28
  27.7 0.0 all-gather.2.cloned.1.call-update
  27.7 0.2 reduce-scatter.2.cloned.1.call-start
  27.9 11.7 %all-gather.2.cloned.1.call-done = bf16[64,8192]{1,0:T(8,128)(2,1)} async-done(((bf16[32,8192]{1,0:T(8,128)(2,1)}), bf16[64,8192]{1,0:T(8,128)(2,1)}) %all-gather.2.cloned.1.call-update) | async-done | bytes 1048592 | tf_op jit(solution)/shard_map/all_gather | solution.py:33
  39.6 1.5 reshape.22
  41.1 6.4 convolution_convert_fusion
  47.5 0.1 reshape.23
  47.6 0.7 copy.7
  48.3 0.0 copy-done
  48.3 26.9 %fusion.11 = f32[3072,6144]{1,0:T(8,128)} fusion(bf16[64,3072]{0,1:T(8,128)(2,1)S(1)} %bitcast.38, bf16[64,6144]{1,0:T(8,128)(2,1)S(1)} %copy-done), kind=kOutput, calls=%fused_computation.18 | convolution fusion | flops 2415919104 | bytes 76677120 | tf_op jit(solution)/shard_map/dot_general | solution.py:39
  75.2 0.0 reduce-scatter.2.cloned.1.call-update
  75.2 1036.7 %reduce-scatter.2.cloned.1.call-done = f32[192,6144]{1,0:T(8,128)} async-done(((f32[3072,6144]{1,0:T(8,128)}), f32[192,6144]{1,0:T(8,128)}) %reduce-scatter.2.cloned.1.call-update) | async-done | bytes 4718608 | tf_op jit(solution)/shard_map/reduce_scatter | solution.py:38
  1111.9 2.6 convert_element_type.30
  1114.6 3.0 reshape.25
  1117.6 4.7 copy.24
Async XLA Ops:
  6.5 41.8 %copy-start = (bf16[64,6144]{1,0:T(8,128)(2,1)S(1)}, bf16[64,6144]{1,0:T(8,128)(2,1)}, u32[]{:S(2)}) copy-start(bf16[64,6144]{1,0:T(8,128)(2,1)} %param.9) | copy-start | bytes 2359300
  6.5 33.1 %all-gather.2.cloned.1.call-start = ((), (), s32[]{:S(2)}) async-start(), calls=%async_computation.1 | async-start | bytes 1572864 | tf_op jit(solution)/shard_map/all_gather | solution.py:33
  27.7 1084.2 %reduce-scatter.2.cloned.1.call-start = ((), (), s32[]{:S(2)}) async-start(), calls=%async_computation.2 | async-start | bytes 80216064 | tf_op jit(solution)/shard_map/reduce_scatter | solution.py:38
Sparse Core Ops, SparseCore 0:
  27.8 11.7 all-gather.1
  75.3 1036.5 reduce-scatter.1
where the time goes:
time: 1130 us
  waiting for transfers between devices  1050 us (93%)
  matrix products  38.6 us (3%)
  local copies, waits for them, and re-layouts  25.8 us (2%)
  between operations  13.5 us (1%)
    reduce_scatter x1, waiting for transfers between devices, per_device(): lax.psum_scatter(lax.dot_general(factor, stored, (((0,), (0,)), ((), ()))...  1040 us
    dot_general x1, matrix products, per_device(): lax.dot_general(factor, stored, (((0,), (0,)), ((), ())), preferred_eleme...  26.9 us
  transfers between devices with their start and end apart: 2, of which 2 were waited for; matrix products, arithmetic and copies ran while one was open for 0% of the time, Pallas kernels for 0%

commit v1 on v0

v1 whole, which is shorter than its diff:
```python
import functools

import jax
import jax.numpy as jnp
from jax import lax
from jax.experimental import pallas as pl
from jax.experimental.pallas import tpu as pltpu
from jax.sharding import PartitionSpec as P

MESH = pl.DeviceIdType.MESH
LANES = 128
PLANE = 4


def contract_kernel(blk, integrals, weights, out):
    nocc = weights.shape[0]
    for p in range(integrals.shape[0]):
        for i in range(nocc):
            total = None
            for t in range(integrals.shape[2] // LANES):
                cols = slice(t * LANES, (t + 1) * LANES)
                term = integrals[p, :, cols].astype(jnp.float32) * weights[i, :, cols]
                total = term if total is None else total + term
            part = total[:, :blk]
            for f in range(1, LANES // blk):
                part = part + total[:, f * blk:(f + 1) * blk]
            out[i, p] = part.astype(out.dtype)


def contract(integrals, weights, blk):
    aux_rows, nb, flat = integrals.shape
    nocc = weights.shape[0]
    step = 8
    return pl.pallas_call(
        functools.partial(contract_kernel, blk),
        grid=(aux_rows // step,),
        in_specs=[
            pl.BlockSpec((step, nb, flat), lambda p: (p, 0, 0)),
            pl.BlockSpec((nocc, nb, flat), lambda p: (0, 0, 0)),
        ],
        out_specs=pl.BlockSpec((nocc, step, nb, blk), lambda p: (0, p, 0, 0)),
        out_shape=jax.ShapeDtypeStruct((nocc, aux_rows, nb, blk), jnp.bfloat16),
    )(integrals, weights)


def factor_kernel(group, columns, parts, *refs):
    del columns
    slabs, out, total = refs[:group], refs[group], refs[group + 1]
    step = pl.program_id(1)

    @pl.when(step == 0)
    def _():
        total[...] = jnp.zeros_like(total)

    acc = total[...]
    for q in range(group):
        acc += jnp.dot(parts[0, q], slabs[q][...], preferred_element_type=jnp.float32)
    total[...] = acc

    @pl.when(step == pl.num_programs(1) - 1)
    def _():
        out[0] = acc.astype(out.dtype)


def factors(parts, columns, virtual):
    shards, nb, rows, blk = parts.shape
    slab = virtual.shape[1]
    group = 8
    slab_specs = [
        pl.BlockSpec((blk, slab), lambda s, k, idx, q=q: (idx[s * nb + k * group + q], 0))
        for q in range(group)
    ]
    return pl.pallas_call(
        functools.partial(factor_kernel, group),
        grid_spec=pltpu.PrefetchScalarGridSpec(
            num_scalar_prefetch=1,
            grid=(shards, nb // group),
            in_specs=[pl.BlockSpec((1, group, rows, blk), lambda s, k, idx: (s, k, 0, 0))]
            + slab_specs,
            out_specs=pl.BlockSpec((1, rows, slab), lambda s, k, idx: (s, 0, 0)),
            scratch_shapes=[pltpu.VMEM((rows, slab), jnp.float32)],
        ),
        out_shape=jax.ShapeDtypeStruct((shards, rows, slab), jnp.bfloat16),
    )(columns, parts, *([virtual] * group))


def panel_kernel(n_aux, n_grp, stored, chunk, out, rows, fac, total, block,
                 own_sem, recv, send, frecv, fsend, precv, psend, orecv, osend):
    me = lax.axis_index("aux")
    grp = lax.axis_index("grp")
    line = n_aux // PLANE
    width = rows.shape[2]
    cut = width // 3 // LANES * LANES
    spans = ((0, cut), (cut, width - cut))
    z = me // PLANE
    su = 1 + grp % 2
    sv = 3 - su
    u = (me // su) % 2
    v = (me // sv) % 2
    next_u = me + su * (1 - 2 * u)
    next_v = me + sv * (1 - 2 * v)
    up, down = z + 1 < line, z >= 1
    targets = {"up": me + PLANE, "down": me - PLANE, "u": next_u, "v": next_v}
    slots = {"up": 0, "down": 1, "u": 2, "v": 3}

    load = pltpu.make_async_copy(
        stored.at[:, pl.ds(pl.multiple_of(grp * width, LANES), width)], rows.at[me], own_sem.at[0])
    load.start()
    mine = pltpu.make_async_copy(chunk.at[me], fac.at[grp, me], own_sem.at[1])
    mine.start()

    barrier = pltpu.get_barrier_semaphore()
    for o in range(1, n_aux):
        pl.semaphore_signal(barrier, inc=1, device_id=(lax.rem(me + o, n_aux), grp), device_id_type=MESH)
    for o in range(1, n_grp):
        pl.semaphore_signal(barrier, inc=1, device_id=(me, lax.rem(grp + o, n_grp)), device_id_type=MESH)
    pl.semaphore_wait(barrier, n_aux - 1 + n_grp - 1)

    def copy(source, colour, way):
        at = rows.at[source, :, pl.ds(*spans[colour])]
        return pltpu.make_async_remote_copy(
            src_ref=at, dst_ref=at,
            send_sem=send.at[colour, slots[way], source], recv_sem=recv.at[colour, source],
            device_id=(targets[way], grp), device_id_type=MESH)

    def when(condition, action):
        if condition is None:
            action()
        else:
            pl.when(condition)(action)

    edges = {"up": up, "down": down, "u": None, "v": None}

    def ways_of(dz, du, dv, colour):
        if dv:
            return ()
        along = ("up", "down") if dz == 0 else (("up",) if dz > 0 else ("down",))
        if colour == 0:
            return ("v",) if du else along + ("u", "v")
        if dz == 0 and du == 0:
            return ("u",) + along + ("v",)
        return along + ("v",)

    def source_of(dz, du, dv):
        return (z - dz) * PLANE + su * (u + du * (1 - 2 * u)) + sv * (v + dv * (1 - 2 * v))

    def valid(dz):
        if dz == 0:
            return None
        return z - dz >= 0 if dz > 0 else z - dz < line

    sent = []

    def forward(dz, du, dv):
        source = source_of(dz, du, dv)
        for colour in (0, 1):
            ways = ways_of(dz, du, dv, colour)
            sent.append((dz, source, colour, ways))

            def act(colour=colour, ways=ways):
                if (dz, du, dv) != (0, 0, 0):
                    copy(source, colour, "v").wait_recv()
                for way in ways:
                    when(edges[way], copy(source, colour, way).start)

            when(valid(dz), act)

    def plane_dot(dz, first):
        def act():
            base = (z - dz) * PLANE
            tile = 512 if width % 512 == 0 else LANES

            @pl.loop(0, width // tile)
            def _(t):
                cols = pl.ds(pl.multiple_of(t * tile, tile), tile)
                right = rows[pl.ds(base, PLANE), :, cols].reshape(-1, tile)
                for q in range(n_grp):
                    left = fac[q, pl.ds(base, PLANE)].reshape(-1, fac.shape[3])
                    term = lax.dot_general(
                        left, right, (((0,), (0,)), ((), ())), preferred_element_type=jnp.float32)
                    if first:
                        total[q, :, cols] = term
                    else:
                        total[q, :, cols] += term

        when(valid(dz), act)

    offsets = [(dz, du, dv) for dz in range(1 - line, line) for du in (0, 1) for dv in (0, 1)]
    hops = lambda o: abs(o[0]) + o[1] + o[2]
    last_hop = line + 1

    def fac_copy(o):
        to = lax.rem(me + o, n_aux)
        return pltpu.make_async_remote_copy(
            src_ref=chunk.at[to], dst_ref=fac.at[grp, me], send_sem=fsend.at[o], recv_sem=frecv.at[o],
            device_id=(to, grp), device_id_type=MESH)

    def fac_wait(o):
        source = lax.rem(me + n_aux - o, n_aux)
        pltpu.make_async_remote_copy(
            src_ref=chunk.at[0], dst_ref=fac.at[grp, source], send_sem=fsend.at[o], recv_sem=frecv.at[o],
            device_id=(source, grp), device_id_type=MESH).wait_recv()
        return source

    def share(o, source, p):
        return pltpu.make_async_remote_copy(
            src_ref=fac.at[grp, source], dst_ref=fac.at[grp, source],
            send_sem=psend.at[p, o], recv_sem=precv.at[p, o],
            device_id=(me, lax.rem(grp + p, n_grp)), device_id_type=MESH)

    for hop in range(last_hop + 1):
        if hop == 0:
            load.wait()
        for offset in offsets:
            if hops(offset) == hop:
                forward(*offset)
        if hop == 0:
            for o in range(1, n_aux):
                fac_copy(o).start()
            mine.wait()
        if hop == 1:
            for o in range(n_aux):
                source = me if o == 0 else fac_wait(o)
                for p in range(1, n_grp):
                    share(o, source, p).start()
            for o in range(n_aux):
                source = lax.rem(me + n_aux - o, n_aux)
                for p in range(1, n_grp):
                    giver = lax.rem(grp + n_grp - p, n_grp)
                    pltpu.make_async_remote_copy(
                        src_ref=fac.at[grp, source], dst_ref=fac.at[giver, source],
                        send_sem=psend.at[p, o], recv_sem=precv.at[p, o],
                        device_id=(me, giver), device_id_type=MESH).wait_recv()
        if hop >= 2:
            for dz in sorted({hop - 2, 2 - hop}):
                plane_dot(dz, hop == 2)

    def give(p):
        to = lax.rem(grp + p, n_grp)
        return pltpu.make_async_remote_copy(
            src_ref=block.at[to], dst_ref=out.at[grp], send_sem=osend.at[p], recv_sem=orecv.at[p],
            device_id=(me, to), device_id_type=MESH)

    for p in range(1, n_grp):
        to = lax.rem(grp + p, n_grp)
        block[to] = total[to].astype(block.dtype)
        give(p).start()
    block[grp] = total[grp].astype(block.dtype)
    keep = pltpu.make_async_copy(block.at[grp], out.at[grp], own_sem.at[2])
    keep.start()

    for dz, source, colour, ways in sent:
        def drain(source=source, colour=colour, ways=ways):
            for way in ways:
                when(edges[way], copy(source, colour, way).wait_send)
        if ways:
            when(valid(dz), drain)
    for o in range(1, n_aux):
        fac_copy(o).wait_send()
    for o in range(n_aux):
        source = lax.rem(me + n_aux - o, n_aux)
        for p in range(1, n_grp):
            share(o, source, p).wait_send()
    for p in range(1, n_grp):
        giver = lax.rem(grp + n_grp - p, n_grp)
        give(p).wait_send()
        pltpu.make_async_remote_copy(
            src_ref=block.at[giver], dst_ref=out.at[giver], send_sem=osend.at[p], recv_sem=orecv.at[p],
            device_id=(me, giver), device_id_type=MESH).wait_recv()
    keep.wait()


def panels(stored, chunk, n_aux, n_grp):
    depth = stored.shape[0]
    width = stored.shape[1] // n_grp
    cols = chunk.shape[2]
    dma = pltpu.SemaphoreType.DMA
    return pl.pallas_call(
        functools.partial(panel_kernel, n_aux, n_grp),
        out_shape=jax.ShapeDtypeStruct((n_grp, cols, width), jnp.bfloat16),
        in_specs=[pl.BlockSpec(memory_space=pltpu.HBM)] * 2,
        out_specs=pl.BlockSpec(memory_space=pltpu.HBM),
        scratch_shapes=[
            pltpu.VMEM((n_aux, depth, width), jnp.bfloat16),
            pltpu.VMEM((n_grp, n_aux, depth, cols), jnp.bfloat16),
            pltpu.VMEM((n_grp, cols, width), jnp.float32),
            pltpu.VMEM((n_grp, cols, width), jnp.bfloat16),
            dma((3,)),
            dma((2, n_aux)),
            dma((2, 4, n_aux)),
            dma((n_aux,)),
            dma((n_aux,)),
            dma((n_grp, n_aux)),
            dma((n_grp, n_aux)),
            dma((n_grp,)),
            dma((n_grp,)),
        ],
        compiler_params=pltpu.CompilerParams(
            collective_id=0, has_side_effects=True, vmem_limit_bytes=60 * 1024 * 1024),
    )(stored, chunk)


def make_per_device(n_aux, n_grp, v):
    def per_device(integrals, block_pairs, occupied, virtual, stored):
        nocc, nbas = occupied.shape
        aux_rows, nb, flat = integrals.shape
        slab = virtual.shape[1]
        local = slab // n_aux
        blk = 1
        while blk * blk < flat:
            blk *= 2
        pairs = block_pairs[0]
        columns = lax.all_gather(pairs[:, 1], "grp", axis=0, tiled=True)
        pick = (pairs[:, 0:1] == jnp.arange(nbas // blk, dtype=jnp.int32)[None, :])
        picked = jnp.einsum(
            "ikm,bk->ibm", occupied.reshape(nocc, nbas // blk, blk), pick.astype(jnp.bfloat16),
            preferred_element_type=jnp.float32)
        weights = jnp.broadcast_to(picked[..., None], (nocc, nb, blk, blk)).reshape(nocc, nb, flat)
        part = contract(integrals, weights, blk)
        part = part.transpose(2, 0, 1, 3).reshape(1, nb, nocc * aux_rows, blk)
        parts = lax.all_gather(part, "grp", axis=0, tiled=True)
        product = factors(parts, columns, virtual)
        chunk = product.reshape(n_grp, nocc, aux_rows, n_aux, local).transpose(3, 0, 2, 1, 4)
        chunk = chunk.reshape(n_aux, n_grp * aux_rows, nocc * local)
        panel = panels(stored, chunk, n_aux, n_grp)
        panel = panel.transpose(1, 0, 2).reshape(nocc, local, n_grp * panel.shape[2] // v, v)
        return panel

    return per_device


def solution(mesh):
    n_aux, n_grp = mesh.shape["aux"], mesh.shape["grp"]

    def whole(integrals, block_pairs, occupied, virtual, stored):
        return jax.shard_map(
            make_per_device(n_aux, n_grp, virtual.shape[1]),
            mesh=mesh,
            in_specs=(
                P(("aux", "grp"), None, None),
                P(("aux", "grp"), None, None),
                P(),
                P(None, "grp"),
                P("aux", None),
            ),
            out_specs=P(None, ("grp", "aux"), None, None),
            check_vma=False,
        )(integrals, block_pairs, occupied, virtual, stored)

    return whole
```

time: 1130 us -> 102 us (0.09)
  waiting for transfers between devices: 1050 us -> 0 us
  Pallas kernels: 0 us -> 81.7 us
  matrix products: 38.6 us -> 0.19 us
  between operations: 13.5 us -> 0.69 us
    reduce_scatter x1 -> x0, waiting for transfers between devices: 1040 us -> none  [per_device(): lax.psum_scatter(lax.dot_general(factor, stored, (((0,), (0,)), ((), ()))...]
    pallas_call x0 -> x3, Pallas kernels: none -> 81.7 us  [the longest x1 70.3 us: panels(): pl.pallas_call(functools.partial(panel_kernel, n_aux, n_grp), out_shape=j...]
    dot_general x5 -> x1, matrix products: 38.6 us -> 0.19 us  [per_device(): jnp.einsum('ikm,bk->ibm', occupied.reshape(nocc, nbas // blk, blk), pick....]
    reshape x7, local copies, waits for them, and re-layouts: 23.4 us -> 11.6 us  [the longest x1 5.5 us: per_device(): panel.transpose(1, 0, 2)]
    all_gather x1 -> x0, waiting for transfers between devices: 11.7 us -> none  [per_device(): piece = lax.all_gather(half, 'grp', axis=0, tiled=True)]
  transfers between devices with their start and end apart: 2 -> 0, of which waited for: 2 -> 0; matrix products, arithmetic and copies ran while one was open for 0% -> 0% of each run, Pallas kernels for 0% -> 0%
where the time goes in v1:
time: 102 us
  Pallas kernels  81.7 us (80%)
  local copies, waits for them, and re-layouts  14.6 us (14%)
  blocking collectives  4.87 us (5%)
    pallas_call x1, Pallas kernels, panels(): pl.pallas_call(functools.partial(panel_kernel, n_aux, n_grp), out_shape=j...  70.3 us
    pallas_call x1, Pallas kernels, factors(): pl.pallas_call(functools.partial(factor_kernel, group), grid_spec=pltpu.P...  6.46 us
    reshape x1, local copies, waits for them, and re-layouts, per_device(): panel.transpose(1, 0, 2)  5.5 us
    pallas_call x1, Pallas kernels, contract(): pl.pallas_call(functools.partial(contract_kernel, blk), grid=(aux_rows //...  4.85 us
    all_gather x1, blocking collectives, per_device(): columns = lax.all_gather(pairs[:, 1], 'grp', axis=0, tiled=True)  2.55 us
    all_gather x1, blocking collectives, per_device(): parts = lax.all_gather(part, 'grp', axis=0, tiled=True)  2.31 us

profile of v1, /device:TPU:0, one launch (start us, length us, event | category | flops | bytes accessed | tf_op | source)
XLA Modules:
  0.0 102.0 jit_solution(11061240159553411120)
XLA Ops:
  0.0 1.2 %dynamic-slice = u32[1]{0:T(128)} dynamic-slice(u32[32]{0:T(128)} %constant.3, u32[]{:T(128)S(6)} %add), dynamic_slice_sizes={1} | dynamic-slice | bytes 12
  1.9 0.7 slice_bitcast_fusion
  2.6 0.8 bitcast_dynamic-update-slice_fusion
  3.3 2.6 %all-reduce.columns = s32[32]{0:T(128)} all-reduce(s32[32]{0:T(128)S(1)} %bitcast_dynamic-update-slice_fusion), channel_id=2, replica_groups=mesh['aux'=16,'grp'=2] {'grp'}, use_global_device_ids=true, to_apply=%add | all-reduce | flops 32 | bytes 256 | tf_op jit(solution)/shard_map/all_gather | solution.py:313
  5.9 0.8 reshape.19
  6.7 0.2 convolution_bitcast_fusion
  6.9 0.3 broadcast_in_dim.2
  7.2 1.2 %reshape.20.weights = f32[2,16,4096]{2,1,0:T(8,128)} reshape(f32[2,16,64,64]{3,2,1,0:T(8,128)S(1)} %broadcast_in_dim.2) | data formatting | bytes 1048576 | tf_op jit(solution)/shard_map/reshape | solution.py:318
  8.4 4.9 %shard_map.55 = bf16[2,32,16,64]{3,2,1,0:T(8,128)(2,1)} custom-call(bf16[32,16,4096]{2,1,0:T(8,128)(2,1)} %integrals.1, f32[2,16,4096]{2,1,0:T(8,128)} %reshape.20.weights), custom_call_target="tpu_custom_call" | custom-call | tf_op jit(solution)/shard_map/pallas_call | solution.py:34
  13.2 1.0 copy.9
  14.3 2.3 %all_gather.7.parts = bf16[2,16,64,64]{3,2,1,0:T(8,128)(2,1)} all-gather(bf16[1,16,64,64]{3,2,1,0:T(8,128)(2,1)S(1)} %copy.9), channel_id=1, replica_groups=mesh['aux'=16,'grp'=2] {'grp'}, dimensions={0}, use_global_device_ids=true | all-gather | bytes 393216 | tf_op jit(solution)/shard_map/all_gather | solution.py:321
  16.6 6.5 %shard_map.56 = bf16[2,64,1536]{2,1,0:T(8,128)(2,1)} custom-call(s32[32]{0:T(128)} %all-reduce.columns, bf16[2,16,64,64]{3,2,1,0:T(8,128)(2,1)} %all_gather.7.parts, bf16[4096,1536]{1,0:T(8,128)(2,1)} %refs_7_.1, bf16[4096,1536]{1,0:T(8,128)(2,1)} %refs_7_.1, bf16[4096,1536]{1,0:T(8,128)(2,1)} %refs_7_.1, bf16[4096,1536]{1,0:T(8,128)(2,1)} %refs_7_.1, ...), custom_call_target="tpu_custom_call" | custom-call | tf_op jit(solution)/shard_map/pallas_call | solution.py:73
  23.0 1.4 %reshape.22 = bf16[2,2,32,16,96]{4,3,2,1,0:T(8,128)(2,1)S(1)} reshape(bf16[2,64,1536]{2,1,0:T(8,128)(2,1)} %shard_map.56) | data formatting | bytes 786432 | tf_op jit(solution)/shard_map/reshape | solution.py:323
  24.5 0.5 copy.13
  25.0 1.1 %reshape.23.chunk = bf16[16,64,192]{2,1,0:T(8,128)(2,1)} reshape(bf16[16,2,32,2,96]{4,3,2,1,0:T(2,128)(2,1)S(1)} %bitcast.24) | data formatting | bytes 786432 | tf_op jit(solution)/shard_map/reshape | solution.py:324
  26.1 70.3 %shard_map.57 = bf16[2,192,3072]{2,1,0:T(8,128)(2,1)} custom-call(bf16[64,6144]{1,0:T(8,128)(2,1)} %stored.1, bf16[16,64,192]{2,1,0:T(8,128)(2,1)} %reshape.23.chunk), custom_call_target="tpu_custom_call" | custom-call | tf_op jit(solution)/shard_map/pallas_call | solution.py:278
  96.5 5.5 %copy.11 = bf16[2,96,2,3072]{3,2,1,0:T(2,128)(2,1)} copy(bf16[2,96,2,3072]{3,1,0,2:T(8,128)(2,1)} %bitcast.23) | data formatting | bytes 4718592 | tf_op jit(solution)/shard_map/reshape | solution.py:326
  (1 shorter events, 0.0 us)

commit v2 on v1

--- a/solution.py
+++ b/solution.py
@@ -1,4 +1,5 @@
 import functools
+import math
 
 import jax
 import jax.numpy as jnp
@@ -12,80 +13,79 @@
 PLANE = 4
 
 
-def contract_kernel(blk, integrals, weights, out):
+def weigh(pairs, occ, weights):
+    nb = pairs.shape[0]
+    nocc, nblocks, blk = occ.shape
+    lanes = lax.broadcasted_iota(jnp.int32, (nb, nblocks), 1)
+    pick = (pairs[:, 0:1] == lanes).astype(jnp.bfloat16)
+    step = 8 * LANES
+    row = lax.broadcasted_iota(jnp.int32, (blk, step), 0) * blk
+    col = lax.broadcasted_iota(jnp.int32, (blk, step), 1)
+    for i in range(nocc):
+        picked = jnp.dot(pick, occ[i], preferred_element_type=jnp.float32).astype(jnp.bfloat16)
+        for t in range(weights.shape[2] // step):
+            offset = col + t * step - row
+            spread = ((offset >= 0) & (offset < blk)).astype(jnp.bfloat16)
+            weights[i, :, t * step:(t + 1) * step] = jnp.dot(
+                picked, spread, preferred_element_type=jnp.float32)
+
+
+def contract(blk, integrals, weights, part):
+    aux_rows = integrals.shape[0]
     nocc = weights.shape[0]
-    for p in range(integrals.shape[0]):
+
+    @pl.loop(0, aux_rows)
+    def _(p):
         for i in range(nocc):
-            total = None
+            sums = [None, None]
             for t in range(integrals.shape[2] // LANES):
                 cols = slice(t * LANES, (t + 1) * LANES)
                 term = integrals[p, :, cols].astype(jnp.float32) * weights[i, :, cols]
-                total = term if total is None else total + term
-            part = total[:, :blk]
+                sums[t % 2] = term if sums[t % 2] is None else sums[t % 2] + term
+            total = sums[0] + sums[1]
+            whole = total
             for f in range(1, LANES // blk):
-                part = part + total[:, f * blk:(f + 1) * blk]
-            out[i, p] = part.astype(out.dtype)
-
-
-def contract(integrals, weights, blk):
-    aux_rows, nb, flat = integrals.shape
-    nocc = weights.shape[0]
-    step = 8
-    return pl.pallas_call(
-        functools.partial(contract_kernel, blk),
-        grid=(aux_rows // step,),
-        in_specs=[
-            pl.BlockSpec((step, nb, flat), lambda p: (p, 0, 0)),
-            pl.BlockSpec((nocc, nb, flat), lambda p: (0, 0, 0)),
-        ],
-        out_specs=pl.BlockSpec((nocc, step, nb, blk), lambda p: (0, p, 0, 0)),
-        out_shape=jax.ShapeDtypeStruct((nocc, aux_rows, nb, blk), jnp.bfloat16),
-    )(integrals, weights)
-
-
-def factor_kernel(group, columns, parts, *refs):
-    del columns
-    slabs, out, total = refs[:group], refs[group], refs[group + 1]
-    step = pl.program_id(1)
-
-    @pl.when(step == 0)
-    def _():
-        total[...] = jnp.zeros_like(total)
-
-    acc = total[...]
-    for q in range(group):
-        acc += jnp.dot(parts[0, q], slabs[q][...], preferred_element_type=jnp.float32)
-    total[...] = acc
-
-    @pl.when(step == pl.num_programs(1) - 1)
-    def _():
-        out[0] = acc.astype(out.dtype)
-
-
-def factors(parts, columns, virtual):
-    shards, nb, rows, blk = parts.shape
-    slab = virtual.shape[1]
-    group = 8
-    slab_specs = [
-        pl.BlockSpec((blk, slab), lambda s, k, idx, q=q: (idx[s * nb + k * group + q], 0))
-        for q in range(group)
-    ]
-    return pl.pallas_call(
-        functools.partial(factor_kernel, group),
-        grid_spec=pltpu.PrefetchScalarGridSpec(
-            num_scalar_prefetch=1,
-            grid=(shards, nb // group),
-            in_specs=[pl.BlockSpec((1, group, rows, blk), lambda s, k, idx: (s, k, 0, 0))]
-            + slab_specs,
-            out_specs=pl.BlockSpec((1, rows, slab), lambda s, k, idx: (s, 0, 0)),
-            scratch_shapes=[pltpu.VMEM((rows, slab), jnp.float32)],
-        ),
-        out_shape=jax.ShapeDtypeStruct((shards, rows, slab), jnp.bfloat16),
-    )(columns, parts, *([virtual] * group))
-
-
-def panel_kernel(n_aux, n_grp, stored, chunk, out, rows, fac, total, block,
-                 own_sem, recv, send, frecv, fsend, precv, psend, orecv, osend):
+                whole = whole + pltpu.roll(total, f * blk, 1)
+            part[i * aux_rows + p] = whole
+
+
+def place(blk, pairs, part, turned, half, grp):
+    nb = pairs.shape[0]
+    per = LANES // blk
+    for k in range(nb):
+        turned[k] = part[:, k, :]
+    lane = lax.broadcasted_iota(jnp.int32, (1, LANES), 1) // blk
+
+    @pl.loop(0, half.shape[2] // LANES)
+    def _(b):
+        here = lane + b * per
+        total = None
+        for k in range(nb):
+            term = jnp.where(here == pairs[k:k + 1, 1:2], turned[k], 0.0)
+            total = term if total is None else total + term
+        half[grp, :, pl.ds(pl.multiple_of(b * LANES, LANES), LANES)] = total.astype(half.dtype)
+
+
+def multiply(nocc, local, half, virt, chunk):
+    n_grp, both, nbas = half.shape
+    aux_rows = both // nocc
+    step = math.lcm(local, LANES)
+    for t in range(virt.shape[1] // step):
+        product = jnp.dot(
+            half[...].reshape(n_grp * both, nbas), virt[:, t * step:(t + 1) * step],
+            preferred_element_type=jnp.float32)
+        for c in range(step // local):
+            d = t * (step // local) + c
+            for q in range(n_grp):
+                for i in range(nocc):
+                    top = q * both + i * aux_rows
+                    chunk[d, q * aux_rows:(q + 1) * aux_rows, i * local:(i + 1) * local] = product[
+                        top:top + aux_rows, c * local:(c + 1) * local].astype(chunk.dtype)
+
+
+def panel_kernel(n_aux, n_grp, integrals, pairs, occ, virtual, stored, out, rows, fac, total, block,
+                 ints, virt, weights, part, turned, half, chunk,
+                 own_sem, recv, send, frecv, fsend, precv, psend, orecv, osend, hrecv, hsend):
     me = lax.axis_index("aux")
     grp = lax.axis_index("grp")
     line = n_aux // PLANE
@@ -107,7 +107,12 @@
         stored.at[:, pl.ds(pl.multiple_of(grp * width, LANES), width)], rows.at[me], own_sem.at[0])
     load.start()
     mine = pltpu.make_async_copy(chunk.at[me], fac.at[grp, me], own_sem.at[1])
-    mine.start()
+    load_ints = pltpu.make_async_copy(integrals, ints, own_sem.at[3])
+    load_ints.start()
+    load_virt = pltpu.make_async_copy(virtual, virt, own_sem.at[4])
+    load_virt.start()
+    nocc, nblocks, blk = occ.shape
+    local = virtual.shape[1] // n_aux
 
     barrier = pltpu.get_barrier_semaphore()
     for o in range(1, n_aux):
@@ -208,6 +213,11 @@
             send_sem=psend.at[p, o], recv_sem=precv.at[p, o],
             device_id=(me, lax.rem(grp + p, n_grp)), device_id_type=MESH)
 
+    def half_copy(p):
+        return pltpu.make_async_remote_copy(
+            src_ref=half.at[grp], dst_ref=half.at[grp], send_sem=hsend.at[p], recv_sem=hrecv.at[p],
+            device_id=(me, lax.rem(grp + p, n_grp)), device_id_type=MESH)
+
     for hop in range(last_hop + 1):
         if hop == 0:
             load.wait()
@@ -215,10 +225,25 @@
             if hops(offset) == hop:
                 forward(*offset)
         if hop == 0:
+            weigh(pairs, occ, weights)
+            load_ints.wait()
+            contract(blk, ints, weights, part)
+            place(blk, pairs, part, turned, half, grp)
+            for p in range(1, n_grp):
+                half_copy(p).start()
+        if hop == 1:
+            for p in range(1, n_grp):
+                giver = lax.rem(grp + n_grp - p, n_grp)
+                pltpu.make_async_remote_copy(
+                    src_ref=half.at[giver], dst_ref=half.at[giver], send_sem=hsend.at[p],
+                    recv_sem=hrecv.at[p], device_id=(me, giver), device_id_type=MESH).wait_recv()
+            load_virt.wait()
+            multiply(nocc, local, half, virt, chunk)
+            mine.start()
             for o in range(1, n_aux):
                 fac_copy(o).start()
             mine.wait()
-        if hop == 1:
+        if hop == 2:
             for o in range(n_aux):
                 source = me if o == 0 else fac_wait(o)
                 for p in range(1, n_grp):
@@ -255,6 +280,8 @@
                 when(edges[way], copy(source, colour, way).wait_send)
         if ways:
             when(valid(dz), drain)
+    for p in range(1, n_grp):
+        half_copy(p).wait_send()
     for o in range(1, n_aux):
         fac_copy(o).wait_send()
     for o in range(n_aux):
@@ -270,22 +297,34 @@
     keep.wait()
 
 
-def panels(stored, chunk, n_aux, n_grp):
+def panels(integrals, pairs, occ, virtual, stored, n_aux, n_grp):
     depth = stored.shape[0]
     width = stored.shape[1] // n_grp
-    cols = chunk.shape[2]
+    aux_rows, nb, flat = integrals.shape
+    nocc, nblocks, blk = occ.shape
+    nbas, slab = virtual.shape
+    cols = nocc * (slab // n_aux)
     dma = pltpu.SemaphoreType.DMA
+    hbm = pl.BlockSpec(memory_space=pltpu.HBM)
+    vmem = pl.BlockSpec(memory_space=pltpu.VMEM)
     return pl.pallas_call(
         functools.partial(panel_kernel, n_aux, n_grp),
         out_shape=jax.ShapeDtypeStruct((n_grp, cols, width), jnp.bfloat16),
-        in_specs=[pl.BlockSpec(memory_space=pltpu.HBM)] * 2,
-        out_specs=pl.BlockSpec(memory_space=pltpu.HBM),
+        in_specs=[hbm, vmem, vmem, hbm, hbm],
+        out_specs=hbm,
         scratch_shapes=[
             pltpu.VMEM((n_aux, depth, width), jnp.bfloat16),
             pltpu.VMEM((n_grp, n_aux, depth, cols), jnp.bfloat16),
             pltpu.VMEM((n_grp, cols, width), jnp.float32),
             pltpu.VMEM((n_grp, cols, width), jnp.bfloat16),
-            dma((3,)),
+            pltpu.VMEM(integrals.shape, jnp.bfloat16),
+            pltpu.VMEM(virtual.shape, jnp.bfloat16),
+            pltpu.VMEM((nocc, nb, flat), jnp.float32),
+            pltpu.VMEM((nocc * aux_rows, nb, LANES), jnp.float32),
+            pltpu.VMEM((nb, nocc * aux_rows, LANES), jnp.float32),
+            pltpu.VMEM((n_grp, nocc * aux_rows, nbas), jnp.bfloat16),
+            pltpu.VMEM((n_aux, depth, cols), jnp.bfloat16),
+            dma((5,)),
             dma((2, n_aux)),
             dma((2, 4, n_aux)),
             dma((n_aux,)),
@@ -294,37 +333,22 @@
             dma((n_grp, n_aux)),
             dma((n_grp,)),
             dma((n_grp,)),
+            dma((n_grp,)),
+            dma((n_grp,)),
         ],
         compiler_params=pltpu.CompilerParams(
-            collective_id=0, has_side_effects=True, vmem_limit_bytes=60 * 1024 * 1024),
-    )(stored, chunk)
+            collective_id=0, has_side_effects=True, vmem_limit_bytes=63 * 1024 * 1024),
+    )(integrals, pairs, occ, virtual, stored)
 
 
 def make_per_device(n_aux, n_grp, v):
     def per_device(integrals, block_pairs, occupied, virtual, stored):
         nocc, nbas = occupied.shape
-        aux_rows, nb, flat = integrals.shape
-        slab = virtual.shape[1]
-        local = slab // n_aux
-        blk = 1
-        while blk * blk < flat:
-            blk *= 2
-        pairs = block_pairs[0]
-        columns = lax.all_gather(pairs[:, 1], "grp", axis=0, tiled=True)
-        pick = (pairs[:, 0:1] == jnp.arange(nbas // blk, dtype=jnp.int32)[None, :])
-        picked = jnp.einsum(
-            "ikm,bk->ibm", occupied.reshape(nocc, nbas // blk, blk), pick.astype(jnp.bfloat16),
-            preferred_element_type=jnp.float32)
-        weights = jnp.broadcast_to(picked[..., None], (nocc, nb, blk, blk)).reshape(nocc, nb, flat)
-        part = contract(integrals, weights, blk)
-        part = part.transpose(2, 0, 1, 3).reshape(1, nb, nocc * aux_rows, blk)
-        parts = lax.all_gather(part, "grp", axis=0, tiled=True)
-        product = factors(parts, columns, virtual)
-        chunk = product.reshape(n_grp, nocc, aux_rows, n_aux, local).transpose(3, 0, 2, 1, 4)
-        chunk = chunk.reshape(n_aux, n_grp * aux_rows, nocc * local)
-        panel = panels(stored, chunk, n_aux, n_grp)
-        panel = panel.transpose(1, 0, 2).reshape(nocc, local, n_grp * panel.shape[2] // v, v)
-        return panel
+        local = virtual.shape[1] // n_aux
+        blk = math.isqrt(integrals.shape[2])
+        occ = occupied.reshape(nocc, nbas // blk, blk)
+        panel = panels(integrals, block_pairs[0], occ, virtual, stored, n_aux, n_grp)
+        return panel.transpose(1, 0, 2).reshape(nocc, local, n_grp * panel.shape[2] // v, v)
 
     return per_device
 

time: 102 us -> 79.7 us (0.78)
  Pallas kernels: 81.7 us -> 71.1 us
  local copies, waits for them, and re-layouts: 14.6 us -> 8.27 us
  blocking collectives: 4.87 us -> 0 us
    pallas_call x2 -> x0, Pallas kernels: 11.3 us -> none  [the longest x1 6.46 us: factors(): pl.pallas_call(functools.partial(factor_kernel, group), grid_spec=pltpu.P...]
    all_gather x2 -> x0, blocking collectives: 4.87 us -> none  [the longest x1 2.55 us: per_device(): columns = lax.all_gather(pairs[:, 1], 'grp', axis=0, tiled=True)]
    reshape x6 -> x1, local copies, waits for them, and re-layouts: 6.08 us -> 1.43 us  [per_device(): occ = occupied.reshape(nocc, nbas // blk, blk)]
    unnamed x3 -> x0, local copies, waits for them, and re-layouts: 2 us -> none
    squeeze x0 -> x1, local copies, waits for them, and re-layouts: none -> 1.35 us  [per_device(): block_pairs[0]]
where the time goes in v2:
time: 79.7 us; the launch traced here: 79.4 us
  Pallas kernels  71.1 us (89%)
  local copies, waits for them, and re-layouts  8.27 us (10%)
    pallas_call x1, Pallas kernels, panels(): pl.pallas_call(functools.partial(panel_kernel, n_aux, n_grp), out_shape=j...  71.1 us
    reshape x1, local copies, waits for them, and re-layouts, per_device(): panel.transpose(1, 0, 2)  5.5 us

profile of v2, /device:TPU:0, one launch (start us, length us, event | category | flops | bytes accessed | tf_op | source)
XLA Modules:
  0.0 79.4 jit_solution(12918870547658429977)
XLA Ops:
  0.0 1.3 %copy.6.pairs = s32[16,2]{1,0:T(8,128)} copy(s32[16,2]{0,1:T(2,128)} %bitcast.5) | data formatting | bytes 256 | tf_op jit(solution)/shard_map/squeeze | solution.py:350
  1.3 1.4 %reshape.6.occ = bf16[2,64,64]{2,1,0:T(8,128)(2,1)} reshape(bf16[2,4096]{1,0:T(2,128)(2,1)} %param.7) | data formatting | bytes 32768 | tf_op jit(solution)/shard_map/reshape | solution.py:349
  2.8 71.1 %shard_map.55 = bf16[2,192,3072]{2,1,0:T(8,128)(2,1)} custom-call(bf16[32,16,4096]{2,1,0:T(8,128)(2,1)} %integrals.1, s32[16,2]{1,0:T(8,128)} %copy.6.pairs, bf16[2,64,64]{2,1,0:T(8,128)(2,1)} %reshape.6.occ, bf16[4096,1536]{1,0:T(8,128)(2,1)} %virtual.1, bf16[64,6144]{1,0:T(8,128)(2,1)} %stored.1), custom_call_target="tpu_custom_call" | custom-call | tf_op jit(solution)/shard_map/pallas_call | solution.py:310
  73.9 5.5 %copy.7 = bf16[2,96,2,3072]{3,2,1,0:T(2,128)(2,1)} copy(bf16[2,96,2,3072]{3,1,0,2:T(8,128)(2,1)} %bitcast.4) | data formatting | bytes 4718592 | tf_op jit(solution)/shard_map/reshape | solution.py:351

commit v3 on v2

--- a/solution.py
+++ b/solution.py
@@ -11,6 +11,14 @@
 MESH = pl.DeviceIdType.MESH
 LANES = 128
 PLANE = 4
+PIECES = 3
+FIRST = 1
+
+
+def spans_of(width):
+    piece = width // PIECES // LANES * LANES
+    starts = [n * piece for n in range(PIECES)] + [width]
+    return [(a, b - a, 0 if n < FIRST else 1) for n, (a, b) in enumerate(zip(starts, starts[1:]))]
 
 
 def weigh(pairs, occ, weights):
@@ -83,15 +91,14 @@
                         top:top + aux_rows, c * local:(c + 1) * local].astype(chunk.dtype)
 
 
-def panel_kernel(n_aux, n_grp, integrals, pairs, occ, virtual, stored, out, rows, fac, total, block,
+def panel_kernel(n_aux, n_grp, integrals, pairs_in, occ, virtual, stored, out, rows, fac, total, block,
                  ints, virt, weights, part, turned, half, chunk,
                  own_sem, recv, send, frecv, fsend, precv, psend, orecv, osend, hrecv, hsend):
     me = lax.axis_index("aux")
     grp = lax.axis_index("grp")
     line = n_aux // PLANE
     width = rows.shape[2]
-    cut = width // 3 // LANES * LANES
-    spans = ((0, cut), (cut, width - cut))
+    spans = spans_of(width)
     z = me // PLANE
     su = 1 + grp % 2
     sv = 3 - su
@@ -111,6 +118,7 @@
     load_ints.start()
     load_virt = pltpu.make_async_copy(virtual, virt, own_sem.at[4])
     load_virt.start()
+    pairs = pairs_in.at[0]
     nocc, nblocks, blk = occ.shape
     local = virtual.shape[1] // n_aux
 
@@ -122,7 +130,7 @@
     pl.semaphore_wait(barrier, n_aux - 1 + n_grp - 1)
 
     def copy(source, colour, way):
-        at = rows.at[source, :, pl.ds(*spans[colour])]
+        at = rows.at[source, :, pl.ds(*spans[colour][:2])]
         return pltpu.make_async_remote_copy(
             src_ref=at, dst_ref=at,
             send_sem=send.at[colour, slots[way], source], recv_sem=recv.at[colour, source],
@@ -158,8 +166,8 @@
 
     def forward(dz, du, dv):
         source = source_of(dz, du, dv)
-        for colour in (0, 1):
-            ways = ways_of(dz, du, dv, colour)
+        for colour in range(len(spans)):
+            ways = ways_of(dz, du, dv, spans[colour][2])
             sent.append((dz, source, colour, ways))
 
             def act(colour=colour, ways=ways):
@@ -260,16 +268,20 @@
             for dz in sorted({hop - 2, 2 - hop}):
                 plane_dot(dz, hop == 2)
 
-    def give(p):
+    def give(p, n):
         to = lax.rem(grp + p, n_grp)
-        return pltpu.make_async_remote_copy(
-            src_ref=block.at[to], dst_ref=out.at[grp], send_sem=osend.at[p], recv_sem=orecv.at[p],
+        cols = pl.ds(*spans[n][:2])
+        return pltpu.make_async_remote_copy(
+            src_ref=block.at[to, :, cols], dst_ref=out.at[grp, :, cols],
+            send_sem=osend.at[p, n], recv_sem=orecv.at[p, n],
             device_id=(me, to), device_id_type=MESH)
 
     for p in range(1, n_grp):
         to = lax.rem(grp + p, n_grp)
-        block[to] = total[to].astype(block.dtype)
-        give(p).start()
+        for n in range(len(spans)):
+            cols = pl.ds(*spans[n][:2])
+            block[to, :, cols] = total[to, :, cols].astype(block.dtype)
+            give(p, n).start()
     block[grp] = total[grp].astype(block.dtype)
     keep = pltpu.make_async_copy(block.at[grp], out.at[grp], own_sem.at[2])
     keep.start()
@@ -290,10 +302,13 @@
             share(o, source, p).wait_send()
     for p in range(1, n_grp):
         giver = lax.rem(grp + n_grp - p, n_grp)
-        give(p).wait_send()
-        pltpu.make_async_remote_copy(
-            src_ref=block.at[giver], dst_ref=out.at[giver], send_sem=osend.at[p], recv_sem=orecv.at[p],
-            device_id=(me, giver), device_id_type=MESH).wait_recv()
+        for n in range(len(spans)):
+            cols = pl.ds(*spans[n][:2])
+            give(p, n).wait_send()
+            pltpu.make_async_remote_copy(
+                src_ref=block.at[giver, :, cols], dst_ref=out.at[giver, :, cols],
+                send_sem=osend.at[p, n], recv_sem=orecv.at[p, n],
+                device_id=(me, giver), device_id_type=MESH).wait_recv()
     keep.wait()
 
 
@@ -303,6 +318,7 @@
     aux_rows, nb, flat = integrals.shape
     nocc, nblocks, blk = occ.shape
     nbas, slab = virtual.shape
+    pieces = len(spans_of(width))
     cols = nocc * (slab // n_aux)
     dma = pltpu.SemaphoreType.DMA
     hbm = pl.BlockSpec(memory_space=pltpu.HBM)
@@ -325,14 +341,14 @@
             pltpu.VMEM((n_grp, nocc * aux_rows, nbas), jnp.bfloat16),
             pltpu.VMEM((n_aux, depth, cols), jnp.bfloat16),
             dma((5,)),
-            dma((2, n_aux)),
-            dma((2, 4, n_aux)),
+            dma((pieces, n_aux)),
+            dma((pieces, 4, n_aux)),
             dma((n_aux,)),
             dma((n_aux,)),
             dma((n_grp, n_aux)),
             dma((n_grp, n_aux)),
-            dma((n_grp,)),
-            dma((n_grp,)),
+            dma((n_grp, pieces)),
+            dma((n_grp, pieces)),
             dma((n_grp,)),
             dma((n_grp,)),
         ],
@@ -347,7 +363,7 @@
         local = virtual.shape[1] // n_aux
         blk = math.isqrt(integrals.shape[2])
         occ = occupied.reshape(nocc, nbas // blk, blk)
-        panel = panels(integrals, block_pairs[0], occ, virtual, stored, n_aux, n_grp)
+        panel = panels(integrals, block_pairs, occ, virtual, stored, n_aux, n_grp)
         return panel.transpose(1, 0, 2).reshape(nocc, local, n_grp * panel.shape[2] // v, v)
 
     return per_device

time: 79.7 us -> 79.4 us (level)
    squeeze x1 -> x0, local copies, waits for them, and re-layouts: 1.35 us -> none  [per_device(): block_pairs[0]]
    unnamed x0 -> x1, local copies, waits for them, and re-layouts: none -> 1.35 us
where the time goes in v3:
time: 79.4 us; the launch traced here: 78.8 us
  Pallas kernels  70.5 us (89%)
  local copies, waits for them, and re-layouts  8.27 us (10%)
    pallas_call x1, Pallas kernels, panels(): pl.pallas_call(functools.partial(panel_kernel, n_aux, n_grp), out_shape=j...  70.5 us
    reshape x1, local copies, waits for them, and re-layouts, per_device(): panel.transpose(1, 0, 2)  5.5 us

profile of v3, /device:TPU:0, one launch (start us, length us, event | category | flops | bytes accessed | tf_op | source)
XLA Modules:
  0.0 78.8 jit_solution(8712741726063751736)
XLA Ops:
  0.0 1.3 %copy.6.pairs_in = s32[1,16,2]{2,1,0:T(8,128)} copy(s32[1,16,2]{1,2,0:T(2,128)} %param.6) | data formatting | bytes 256 | tf_op args[1]
  1.3 1.4 %reshape.6.occ = bf16[2,64,64]{2,1,0:T(8,128)(2,1)} reshape(bf16[2,4096]{1,0:T(2,128)(2,1)} %param.7) | data formatting | bytes 32768 | tf_op jit(solution)/shard_map/reshape | solution.py:365
  2.8 70.5 %shard_map.55 = bf16[2,192,3072]{2,1,0:T(8,128)(2,1)} custom-call(bf16[32,16,4096]{2,1,0:T(8,128)(2,1)} %integrals.1, s32[1,16,2]{2,1,0:T(8,128)} %copy.6.pairs_in, bf16[2,64,64]{2,1,0:T(8,128)(2,1)} %reshape.6.occ, bf16[4096,1536]{1,0:T(8,128)(2,1)} %virtual.1, bf16[64,6144]{1,0:T(8,128)(2,1)} %stored.1), custom_call_target="tpu_custom_call" | custom-call | tf_op jit(solution)/shard_map/pallas_call | solution.py:326
  73.3 5.5 %copy.7 = bf16[2,96,2,3072]{3,2,1,0:T(2,128)(2,1)} copy(bf16[2,96,2,3072]{3,1,0,2:T(8,128)(2,1)} %bitcast.3) | data formatting | bytes 4718592 | tf_op jit(solution)/shard_map/reshape | solution.py:367
